TPU v7x, 32 devices: a whole 2x2x4 slice. The times are simulated.
32 devices in a mesh: dom: 16 (over z, y, x), spin: 2 (over core).
Axes of the slice: x: 2, y: 2, z: 4, core: 2. Of those that a mesh axis runs over, the one named last changes fastest.
Arguments:
- vectors: float32 [2, 8, 262144], P('spin', None, 'dom'), may hold values from -17 to 17
- basis: float32 [2, 16, 262144], P('spin', None, 'dom'), may hold values from -17 to 17
- potential: float32 [2, 262144], P('spin', 'dom'), may hold values from 1 to 3
- hop_table: bfloat16 [8, 128, 128], replicated, may hold values from -0.25 to 0.25
- soc_table: bfloat16 [2, 128, 128], replicated, may hold values from -0.5 to 0.5
- nbr_block: int32 [2048, 16], P('dom'), may hold values from 0 to 2047, as said below
- nbr_type: int32 [2048, 16], P('dom'), may hold values from 0 to 7
- nbr_count: int32 [2048], P('dom'), may hold values from 1 to 16, as said below
- flip_block: int32 [2048], P('dom'), may hold values from 0 to 2047, as said below
Outputs:
- block_one: float32 [2, 8, 262144], P('spin', None, 'dom')
- block_two: float32 [2, 8, 262144], P('spin', None, 'dom')
- coefs_one: float32 [32, 8], replicated
- coefs_two: float32 [40, 8], replicated
Inputs may be any that keep to these rules, and one draw needn't show every extreme that they name: nbr_block[i, l] equals i + d modulo 2048 with -8 <= d <= 8; slots at or beyond nbr_count[i] are ignored; in slot 0, the first block of each group of 128 has d = -8 and the last has d = 8. `nbr_count`: some block has all 16 slots live. flip_block[i] lies in the same domain as i: flip_block[i] // 128 == i // 128.
All inputs are finite; a program needn't handle non-finite values.
Results may differ from a plain program's by a relative error of at most 0.0033.
Values may be sent and summed in bfloat16 or wider, within the bound.
A program may use at most 64 MiB of HBM per device.

v0:
```python
import jax
import jax.numpy as jnp
from jax import lax
from jax.sharding import PartitionSpec as P

RANGE = 8


def extended_2(cells, sides, width):
    for axis, dim in sides:
        count = lax.axis_size(axis)
        head = lax.slice_in_dim(cells, 0, width, axis=dim)
        tail = lax.slice_in_dim(cells, cells.shape[dim] - width, cells.shape[dim], axis=dim)
        cells = jnp.concatenate(
            [
                lax.ppermute(tail, axis, [(i, (i + 1) % count) for i in range(count)]),
                cells,
                lax.ppermute(head, axis, [((i + 1) % count, i) for i in range(count)]),
            ],
            axis=dim,
        )
    return cells


def partner(block, axis, distance):
    count = lax.axis_size(axis)
    route = []
    for low in range(count):
        high = low | 1 << distance
        if high != low and high < count:
            route += [(low, high), (high, low)]
    return lax.ppermute(block, axis, route)


def inner_rows(left_rows, right_rows):
    return lax.dot_general(
        left_rows, right_rows, (((1,), (1,)), ((), ())), precision=lax.Precision.HIGHEST
    )


def times_rows(coef_matrix, span_rows):
    return lax.dot_general(
        coef_matrix, span_rows, (((0,), (0,)), ((), ())), precision=lax.Precision.HIGHEST
    )


def small_product(left_matrix, right_matrix):
    return jnp.dot(left_matrix, right_matrix, precision=lax.Precision.HIGHEST)


def per_device(
    vectors, basis, potential, hop_table, soc_table, nbr_block, nbr_type, nbr_count, flip_block
):
    block_local = nbr_block.shape[0]
    block_width = hop_table.shape[1]
    type_total = hop_table.shape[0]
    slot_total = nbr_block.shape[1]
    vector_count = vectors.shape[1]
    domain_total = lax.axis_size("dom")
    block_total = block_local * domain_total
    norm_count = float(2 * block_local * block_width * domain_total)
    first_block = lax.axis_index("dom") * block_local
    spin_index = lax.axis_index("spin")
    local_index = jnp.arange(block_local, dtype=jnp.int32)
    offset = (nbr_block - (first_block + local_index)[:, None] + RANGE) % block_total - RANGE
    flat_index = (local_index[:, None] + RANGE + offset) * type_total + nbr_type
    live_mask = (jnp.arange(slot_total, dtype=jnp.int32)[None, :] < nbr_count[:, None]).astype(
        jnp.float32
    )
    flip_local = flip_block - first_block
    soc_own = lax.dynamic_index_in_dim(soc_table, spin_index, 0, keepdims=False)
    onsite = potential[0]

    def apply_operator(field):
        rounded = field.reshape(vector_count, block_local, block_width).astype(jnp.bfloat16)
        extended = extended_2(rounded, (("dom", 1),), RANGE)
        products = jnp.einsum(
            "kjc,tbc->kjtb", extended, hop_table, preferred_element_type=jnp.float32
        )
        products = products.reshape(vector_count, -1, block_width)
        gathered = jnp.take(products, flat_index.reshape(-1), axis=1)
        gathered = gathered.reshape(vector_count, block_local, slot_total, block_width)
        hopping = jnp.sum(gathered * live_mask[None, :, :, None], axis=2)
        other_side = partner(rounded, "spin", 0)
        picked = jnp.take(other_side, flip_local, axis=1)
        flip_term = jnp.einsum("kic,bc->kib", picked, soc_own, preferred_element_type=jnp.float32)
        return onsite[None, :] * field + (hopping + flip_term).reshape(vector_count, -1)

    def orthonormal(span, image):
        span_gram, correlation, image_gram = lax.psum(
            (inner_rows(span, span), inner_rows(span, image), inner_rows(image, image)),
            ("dom", "spin"),
        )
        span_gram = span_gram / norm_count
        first_coef = correlation / norm_count
        image_gram = image_gram / norm_count
        total_coef = 2.0 * first_coef - small_product(span_gram, first_coef)
        twice = image - times_rows(total_coef, span)
        gram_matrix = (
            image_gram
            - small_product(total_coef.T, first_coef)
            - small_product(first_coef.T, total_coef)
            + small_product(total_coef.T, small_product(span_gram, total_coef))
        )
        lower_factor = jnp.linalg.cholesky(gram_matrix)
        new_block = lax.linalg.triangular_solve(lower_factor, twice, left_side=True, lower=True)
        coefs = jnp.concatenate([total_coef, lower_factor.T], axis=0)
        return (new_block, coefs)

    current = vectors[0]
    span = jnp.concatenate([basis[0], current], axis=0)
    block_one, coefs_one = orthonormal(span, apply_operator(current))
    span_two = jnp.concatenate([span, block_one], axis=0)
    block_two, coefs_two = orthonormal(span_two, apply_operator(block_one))
    return (block_one[None], block_two[None], coefs_one, coefs_two)


def solution(mesh):
    return jax.shard_map(
        per_device,
        mesh=mesh,
        in_specs=(
            P("spin", None, "dom"),
            P("spin", None, "dom"),
            P("spin", "dom"),
            P(),
            P(),
            P("dom", None),
            P("dom", None),
            P("dom"),
            P("dom"),
        ),
        out_specs=(P("spin", None, "dom"), P("spin", None, "dom"), P(), P()),
        check_vma=False,
    )
```

profile of v0, /device:TPU:0, one launch (start us, length us, event | category | flops | bytes accessed | tf_op | source)
XLA Modules:
  0.0 202.6 jit_solution(12468295660769314962)
XLA Ops:
  0.6 1.2 copy.121
  2.4 2.5 %collective-permute-start = (bf16[8,8,128]{2,1,0:T(8,128)(2,1)S(1)}, bf16[8,8,128]{2,1,0:T(8,128)(2,1)S(1)}, u32[]{:S(2)}, u32[]{:S(2)}) collective-permute-start(bf16[8,8,128]{2,1,0:T(8,128)(2,1)S(1)} %get-tuple-element.18), channel_id=1, source_target_pairs={{0,2},{2,4},{4,6},{6,8},{8,10},{10,12},{12,14},{14,16},{16,18},{18... | collective-permute-start | bytes 49160 | tf_op jit(solution)/shard_map/ppermute | solution.py:16
  5.0 4.1 %collective-permute-start.1 = (bf16[8,8,128]{2,1,0:T(8,128)(2,1)S(1)}, bf16[8,8,128]{2,1,0:T(8,128)(2,1)S(1)}, u32[]{:S(2)}, u32[]{:S(2)}) collective-permute-start(bf16[8,8,128]{2,1,0:T(8,128)(2,1)S(1)} %get-tuple-element.19), channel_id=1, source_target_pairs={{2,0},{4,2},{6,4},{8,6},{10,8},{12,10},{14,12},{16,14},{18,16},{20... | collective-permute-start | bytes 49160 | tf_op jit(solution)/shard_map/ppermute | solution.py:18
  10.7 1.2 compare_and_fusion.1
  11.9 4.2 %fusion.1 = f32[24,24]{1,0:T(8,128)} fusion(f32[8,16384]{1,0:T(8,128)} %bitcast.113, f32[16,16384]{1,0:T(8,128)} %bitcast.122), kind=kOutput, calls=%fused_computation.27 | convolution fusion | flops 113639424 | bytes 1575168 | tf_op jit(solution)/shard_map/dot_general | solution.py:36
  16.1 0.8 fusion.8
  16.8 1.4 copy.120
  18.3 7.5 %copy.57 = f32[8,1152,128]{2,0,1:T(8,128)} copy(f32[8,1152,128]{2,1,0:T(8,128)S(1)} %bitcast.120) | data formatting | bytes 9437184 | tf_op jit(solution)/shard_map/reshape | solution.py:80
  25.8 18.1 %gather_fusion = f32[2048,8,128]{2,1,0:T(8,128)} fusion(f32[8,1152,128]{2,0,1:T(8,128)} %copy.57, s32[2048]{0:T(1024)S(1)} %fusion.43), kind=kCustom, calls=%fused_computation.clone | custom fusion | bytes 16785408 | tf_op jit(solution)/shard_map/jit(_take)/gather | solution.py:81
  43.9 9.2 %multiply_reduce_fusion.1 = f32[8,128,128]{2,0,1:T(8,128)S(1)} fusion(f32[128,16]{1,0:T(8,128)S(1)} %fusion.25, f32[2048,8,128]{2,1,0:T(8,128)} %gather_fusion, pred[2048]{0:T(1024)(128)(4,1)S(1)} %compare_and_fusion), kind=kLoop, calls=%fused_computation.8 | loop fusion | flops 6160384 | bytes 8923136 | tf_op jit(solution)/shard_map/reduce_sum | solution.py:83
  54.0 0.9 select_bitcast_fusion.1
  54.9 1.1 fusion.5
  56.0 1.3 convolution_bitcast_fusion.1
  57.3 1.6 fusion.2
  59.0 38.1 %all-reduce.1 = (f32[24,24]{1,0:T(8,128)S(1)}, f32[24,8]{0,1:T(8,128)S(1)}, f32[8,8]{0,1:T(8,128)S(1)}) all-reduce(f32[24,24]{1,0:T(8,128)S(1)} %copy-done.5, f32[24,8]{0,1:T(8,128)S(1)} %fusion.2, f32[8,8]{0,1:T(8,128)S(1)} %convolution_bitcast_fusion.1), channel_id=1, replica_groups=mesh['dom'=16,'spin'=2] {'dom','spin'}, use_global_device_ids=true, to_apply=%region_3.6 | all-reduce | flops 832 | bytes 6656 | tf_op jit(solution)/shard_map/psum | solution.py:90
  97.4 1.2 convolution_subtract_fusion.1
  102.5 2.4 %fusion.3 = f32[32,32]{1,0:T(8,128)} fusion(f32[8,16384]{1,0:T(8,128)S(1)} %fusion.47, f32[8,16384]{1,0:T(8,128)S(1)} %bitcast.117, f32[16,16384]{1,0:T(8,128)S(1)} %bitcast.125), kind=kOutput, calls=%fused_computation.29 | convolution fusion | flops 202375168 | bytes 2101248 | tf_op jit(solution)/shard_map/dot_general | solution.py:36
  104.9 2.3 %collective-permute-start.3 = (bf16[8,8,128]{2,1,0:T(8,128)(2,1)S(1)}, bf16[8,8,128]{2,1,0:T(8,128)(2,1)S(1)}, u32[]{:S(2)}, u32[]{:S(2)}) collective-permute-start(bf16[8,8,128]{2,1,0:T(8,128)(2,1)S(1)} %get-tuple-element.16), channel_id=1, source_target_pairs={{0,2},{2,4},{4,6},{6,8},{8,10},{10,12},{12,14},{14,16},{16,18},{18... | collective-permute-start | bytes 49160 | tf_op jit(solution)/shard_map/ppermute | solution.py:16
  107.2 3.3 %collective-permute-start.4 = (bf16[8,8,128]{2,1,0:T(8,128)(2,1)S(1)}, bf16[8,8,128]{2,1,0:T(8,128)(2,1)S(1)}, u32[]{:S(2)}, u32[]{:S(2)}) collective-permute-start(bf16[8,8,128]{2,1,0:T(8,128)(2,1)S(1)} %get-tuple-element.17), channel_id=1, source_target_pairs={{2,0},{4,2},{6,4},{8,6},{10,8},{12,10},{14,12},{16,14},{18,16},{20... | collective-permute-start | bytes 49160 | tf_op jit(solution)/shard_map/ppermute | solution.py:18
  111.2 1.0 collective-permute-done.3
  112.2 0.8 fusion.13
  113.0 1.4 copy.119
  114.4 7.5 %copy.73 = f32[8,1152,128]{2,0,1:T(8,128)} copy(f32[8,1152,128]{2,1,0:T(8,128)S(1)} %bitcast.121) | data formatting | bytes 9437184 | tf_op jit(solution)/shard_map/reshape | solution.py:80
  122.0 18.1 %gather_fusion.2 = f32[2048,8,128]{2,1,0:T(8,128)} fusion(f32[8,1152,128]{2,0,1:T(8,128)} %copy.73, s32[2048]{0:T(1024)S(1)} %fusion.43), kind=kCustom, calls=%fused_computation.2.clone | custom fusion | bytes 16785408 | tf_op jit(solution)/shard_map/jit(_take)/gather | solution.py:81
  140.1 9.1 %multiply_reduce_fusion = f32[8,128,128]{2,0,1:T(8,128)S(1)} fusion(f32[128,16]{1,0:T(8,128)S(1)} %fusion.25, f32[2048,8,128]{2,1,0:T(8,128)} %gather_fusion.2, pred[2048]{0:T(1024)(128)(4,1)S(1)} %compare_and_fusion), kind=kLoop, calls=%fused_computation.7 | loop fusion | flops 6160384 | bytes 8923136 | tf_op jit(solution)/shard_map/reduce_sum | solution.py:83
  149.2 1.6 gather_fusion.3
  151.1 1.0 fusion
  152.1 1.3 fusion.7
  153.4 1.9 fusion.4
  155.3 40.4 %all-reduce = (f32[32,32]{1,0:T(8,128)S(1)}, f32[32,8]{0,1:T(8,128)S(1)}, f32[8,8]{0,1:T(8,128)S(1)}) all-reduce(f32[32,32]{1,0:T(8,128)S(1)} %copy-done.6, f32[32,8]{0,1:T(8,128)S(1)} %fusion.4, f32[8,8]{0,1:T(8,128)S(1)} %fusion.7), channel_id=1, replica_groups=mesh['dom'=16,'spin'=2] {'dom','spin'}, use_global_device_ids=true, to_apply=%region_9.14 | all-reduce | flops 1344 | bytes 10752 | tf_op jit(solution)/shard_map/psum | solution.py:90
  196.0 1.3 convolution_subtract_fusion
  201.2 1.4 convolution_bitcast_fusion
  (65 shorter events, 12.4 us)
Async XLA Ops:
  0.6 15.4 %copy-start = (bf16[8,128,128]{2,1,0:T(8,128)(2,1)S(1)}, bf16[8,128,128]{2,1,0:T(8,128)(2,1)}, u32[]{:S(2)}) copy-start(bf16[8,128,128]{2,1,0:T(8,128)(2,1)} %param.19) | copy-start | bytes 786436
  1.8 51.3 %collective-permute-start.2 = (bf16[8,128,128]{2,1,0:T(8,128)(2,1)S(1)}, bf16[8,128,128]{2,1,0:T(8,128)(2,1)S(1)}, u32[]{:S(2)}, u32[]{:S(2)}) collective-permute-start(bf16[8,128,128]{2,1,0:T(8,128)(2,1)S(1)} %bitcast.137), channel_id=1, source_target_pairs={{0,1},{1,0},{2,3},{3,2},{4,5},{5,4},{6,7},{7,6},{8,9},{9,8},{10,11... | collective-permute-start | bytes 786440 | tf_op jit(solution)/shard_map/ppermute | solution.py:32
  2.4 13.6 %collective-permute-start = (bf16[8,8,128]{2,1,0:T(8,128)(2,1)S(1)}, bf16[8,8,128]{2,1,0:T(8,128)(2,1)S(1)}, u32[]{:S(2)}, u32[]{:S(2)}) collective-permute-start(bf16[8,8,128]{2,1,0:T(8,128)(2,1)S(1)} %get-tuple-element.18), channel_id=1, source_target_pairs={{0,2},{2,4},{4,6},{6,8},{8,10},{10,12},{12,14},{14,16},{16,18},{18... | collective-permute-start | bytes 49160 | tf_op jit(solution)/shard_map/ppermute | solution.py:16
  5.0 11.1 %collective-permute-start.1 = (bf16[8,8,128]{2,1,0:T(8,128)(2,1)S(1)}, bf16[8,8,128]{2,1,0:T(8,128)(2,1)S(1)}, u32[]{:S(2)}, u32[]{:S(2)}) collective-permute-start(bf16[8,8,128]{2,1,0:T(8,128)(2,1)S(1)} %get-tuple-element.19), channel_id=1, source_target_pairs={{2,0},{4,2},{6,4},{8,6},{10,8},{12,10},{14,12},{16,14},{18,16},{20... | collective-permute-start | bytes 49160 | tf_op jit(solution)/shard_map/ppermute | solution.py:18
  43.9 11.0 %copy-start.1 = (f32[1,8,16384]{2,1,0:T(8,128)S(1)}, f32[1,8,16384]{2,1,0:T(8,128)}, u32[]{:S(2)}) copy-start(f32[1,8,16384]{2,1,0:T(8,128)} %param.16) | copy-start | bytes 1572868
  43.9 11.0 %copy-start.4 = (f32[1,16384]{1,0:T(1,128)S(1)}, f32[1,16384]{1,0:T(1,128)}, u32[]{:S(2)}) copy-start(f32[1,16384]{1,0:T(1,128)} %param.18) | copy-start | bytes 196612
  53.3 4.0 %copy-start.2 = (f32[1,16,16384]{2,1,0:T(8,128)S(1)}, f32[1,16,16384]{2,1,0:T(8,128)}, u32[]{:S(2)}) copy-start(f32[1,16,16384]{2,1,0:T(8,128)} %param.17) | copy-start | bytes 3145732
  54.9 4.0 %copy-start.5 = (f32[24,24]{1,0:T(8,128)S(1)}, f32[24,24]{1,0:T(8,128)}, u32[]{:S(2)}) copy-start(f32[24,24]{1,0:T(8,128)} %fusion.1) | copy-start | bytes 6916
  102.3 93.7 %copy-start.3 = (f32[8,16384]{1,0:T(8,128)}, f32[8,16384]{1,0:T(8,128)S(1)}, u32[]{:S(2)}) copy-start(f32[8,16384]{1,0:T(8,128)S(1)} %fusion.47) | copy-start | bytes 1572868
  102.4 46.8 %collective-permute-start.5 = (bf16[8,128,128]{2,0,1:T(8,128)(2,1)S(1)}, bf16[8,128,128]{2,0,1:T(8,128)(2,1)}, u32[]{:S(2)}, u32[]{:S(2)}) collective-permute-start(bf16[8,128,128]{2,0,1:T(8,128)(2,1)S(1)} %convert_bitcast_fusion), channel_id=1, source_target_pairs={{0,1},{1,0},{2,3},{3,2},{4,5},{5,4},{6,7},{7,6},{8,9},{9,8},{10,11... | collective-permute-start | bytes 786440 | tf_op jit(solution)/shard_map/ppermute | solution.py:32
  104.9 7.3 %collective-permute-start.3 = (bf16[8,8,128]{2,1,0:T(8,128)(2,1)S(1)}, bf16[8,8,128]{2,1,0:T(8,128)(2,1)S(1)}, u32[]{:S(2)}, u32[]{:S(2)}) collective-permute-start(bf16[8,8,128]{2,1,0:T(8,128)(2,1)S(1)} %get-tuple-element.16), channel_id=1, source_target_pairs={{0,2},{2,4},{4,6},{6,8},{8,10},{10,12},{12,14},{14,16},{16,18},{18... | collective-permute-start | bytes 49160 | tf_op jit(solution)/shard_map/ppermute | solution.py:16
  107.2 5.1 %collective-permute-start.4 = (bf16[8,8,128]{2,1,0:T(8,128)(2,1)S(1)}, bf16[8,8,128]{2,1,0:T(8,128)(2,1)S(1)}, u32[]{:S(2)}, u32[]{:S(2)}) collective-permute-start(bf16[8,8,128]{2,1,0:T(8,128)(2,1)S(1)} %get-tuple-element.17), channel_id=1, source_target_pairs={{2,0},{4,2},{6,4},{8,6},{10,8},{12,10},{14,12},{16,14},{18,16},{20... | collective-permute-start | bytes 49160 | tf_op jit(solution)/shard_map/ppermute | solution.py:18
  140.1 10.8 %copy-start.7 = (pred[128]{0:T(512)(128)(4,1)S(1)}, pred[128]{0:T(512)(128)(4,1)}, u32[]{:S(2)}) copy-start(pred[128]{0:T(512)(128)(4,1)} %get-tuple-element.14) | copy-start | bytes 388
  152.1 3.2 %copy-start.6 = (f32[32,32]{1,0:T(8,128)S(1)}, f32[32,32]{1,0:T(8,128)}, u32[]{:S(2)}) copy-start(f32[32,32]{1,0:T(8,128)} %fusion.3) | copy-start | bytes 12292
where the time goes:
time: 203 us
  blocking collectives  78.6 us (39%)
  local copies, waits for them, and re-layouts  58.3 us (29%)
  other arithmetic  28.8 us (14%)
  matrix products  22.2 us (11%)
  starting transfers between devices  12.9 us (6%)
    psum x2, blocking collectives, orthonormal(): lax.psum((inner_rows(span, span), inner_rows(span, image), inner_rows(ima...  78.6 us
    gather x2, local copies, waits for them, and re-layouts, apply_operator(): gathered = jnp.take(products, flat_index.reshape(-1), axis=1)  36.3 us
    reduce_sum x2, other arithmetic, apply_operator(): hopping = jnp.sum(gathered * live_mask[None, :, :, None], axis=2)  18.3 us
    reshape x2, local copies, waits for them, and re-layouts, apply_operator(): products = products.reshape(vector_count, -1, block_width)  15.1 us
    dot_general x6, matrix products, inner_rows(): lax.dot_general(left_rows, right_rows, (((1,), (1,)), ((), ())), precisio...  12.6 us
    ppermute x2, starting transfers between devices, extended_2(): lax.ppermute(head, axis, [((i + 1) % count, i) for i in range(count)])  7.41 us
    ppermute x2, starting transfers between devices, extended_2(): lax.ppermute(tail, axis, [(i, (i + 1) % count) for i in range(count)])  4.82 us
  transfers between devices with their start and end apart: 6, of which 1 were waited for; matrix products, arithmetic and copies ran while one was open for 42% of the time, Pallas kernels for 0%

commit v1 on v0

--- a/solution.py
+++ b/solution.py
@@ -88,8 +88,10 @@
 
     def orthonormal(span, image):
         span_gram, correlation, image_gram = lax.psum(
-            (inner_rows(span, span), inner_rows(span, image), inner_rows(image, image)),
-            ("dom", "spin"),
+            lax.psum(
+                (inner_rows(span, span), inner_rows(span, image), inner_rows(image, image)), "dom"
+            ),
+            "spin",
         )
         span_gram = span_gram / norm_count
         first_coef = correlation / norm_count

time: 203 us -> 283 us (1.39)
  blocking collectives: 78.6 us -> 158 us
    psum x2, blocking collectives: 78.6 us -> 151 us  [orthonormal(): lax.psum((inner_rows(span, span), inner_rows(span, image), inner_rows(ima...]
    psum x0 -> x2, blocking collectives: none -> 6.99 us  [orthonormal(): lax.psum(lax.psum((inner_rows(span, span), inner_rows(span, image), inner...]
  transfers between devices with their start and end apart: 6 -> 6, of which waited for: 1 -> 1; matrix products, arithmetic and copies ran while one was open for 42% -> 30% of each run, Pallas kernels for 0% -> 0%
where the time goes in v1:
time: 283 us; the launch traced here: 282 us
  blocking collectives  158 us (56%)
  local copies, waits for them, and re-layouts  58.3 us (21%)
  other arithmetic  28.8 us (10%)
  matrix products  22.2 us (8%)
  starting transfers between devices  13.1 us (5%)
    psum x2, blocking collectives, orthonormal(): lax.psum((inner_rows(span, span), inner_rows(span, image), inner_rows(ima...  151 us
    gather x2, local copies, waits for them, and re-layouts, apply_operator(): gathered = jnp.take(products, flat_index.reshape(-1), axis=1)  36.3 us
    reduce_sum x2, other arithmetic, apply_operator(): hopping = jnp.sum(gathered * live_mask[None, :, :, None], axis=2)  18.3 us
    reshape x2, local copies, waits for them, and re-layouts, apply_operator(): products = products.reshape(vector_count, -1, block_width)  15.1 us
    dot_general x6, matrix products, inner_rows(): lax.dot_general(left_rows, right_rows, (((1,), (1,)), ((), ())), precisio...  12.6 us
    ppermute x2, starting transfers between devices, extended_2(): lax.ppermute(head, axis, [((i + 1) % count, i) for i in range(count)])  9.67 us
    psum x2, blocking collectives, orthonormal(): lax.psum(lax.psum((inner_rows(span, span), inner_rows(span, image), inner...  6.99 us
  transfers between devices with their start and end apart: 6, of which 1 were waited for; matrix products, arithmetic and copies ran while one was open for 30% of the time, Pallas kernels for 0%

profile of v1, /device:TPU:0, one launch (start us, length us, event | category | flops | bytes accessed | tf_op | source)
XLA Modules:
  0.0 282.1 jit_solution(6484180604633827378)
XLA Ops:
  0.6 1.2 copy.121
  2.4 2.5 collective-permute-start
  5.0 4.1 %collective-permute-start.1 = (bf16[8,8,128]{2,1,0:T(8,128)(2,1)S(1)}, bf16[8,8,128]{2,1,0:T(8,128)(2,1)S(1)}, u32[]{:S(2)}, u32[]{:S(2)}) collective-permute-start(bf16[8,8,128]{2,1,0:T(8,128)(2,1)S(1)} %get-tuple-element.25), channel_id=1, source_target_pairs={{2,0},{4,2},{6,4},{8,6},{10,8},{12,10},{14,12},{16,14},{18,16},{20... | collective-permute-start | bytes 49160 | tf_op jit(solution)/shard_map/ppermute | solution.py:18
  10.7 1.2 compare_and_fusion.1
  11.9 4.2 %fusion.1 = f32[24,24]{1,0:T(8,128)} fusion(f32[8,16384]{1,0:T(8,128)} %bitcast.113, f32[16,16384]{1,0:T(8,128)} %bitcast.122), kind=kOutput, calls=%fused_computation.27 | convolution fusion | flops 113639424 | bytes 1575168 | tf_op jit(solution)/shard_map/dot_general | solution.py:36
  16.8 1.4 copy.120
  18.3 7.5 %copy.57 = f32[8,1152,128]{2,0,1:T(8,128)} copy(f32[8,1152,128]{2,1,0:T(8,128)S(1)} %bitcast.120) | data formatting | bytes 9437184 | tf_op jit(solution)/shard_map/reshape | solution.py:80
  25.8 18.1 %gather_fusion = f32[2048,8,128]{2,1,0:T(8,128)} fusion(f32[8,1152,128]{2,0,1:T(8,128)} %copy.57, s32[2048]{0:T(1024)S(1)} %fusion.43), kind=kCustom, calls=%fused_computation.clone | custom fusion | bytes 16785408 | tf_op jit(solution)/shard_map/jit(_take)/gather | solution.py:81
  43.9 9.2 %multiply_reduce_fusion.1 = f32[8,128,128]{2,0,1:T(8,128)S(1)} fusion(f32[128,16]{1,0:T(8,128)S(1)} %fusion.25, f32[2048,8,128]{2,1,0:T(8,128)} %gather_fusion, pred[2048]{0:T(1024)(128)(4,1)S(1)} %compare_and_fusion), kind=kLoop, calls=%fused_computation.8 | loop fusion | flops 6160384 | bytes 8923136 | tf_op jit(solution)/shard_map/reduce_sum | solution.py:83
  54.0 0.9 select_bitcast_fusion.1
  54.9 1.1 fusion.5
  56.0 1.3 convolution_bitcast_fusion.1
  57.3 1.6 fusion.2
  59.0 73.5 %all-reduce.1 = (f32[24,24]{1,0:T(8,128)S(1)}, f32[24,8]{0,1:T(8,128)S(1)}, f32[8,8]{0,1:T(8,128)S(1)}) all-reduce(f32[24,24]{1,0:T(8,128)S(1)} %copy-done.5, f32[24,8]{0,1:T(8,128)S(1)} %fusion.2, f32[8,8]{0,1:T(8,128)S(1)} %convolution_bitcast_fusion.1), channel_id=1, replica_groups=mesh['dom'=16,'spin'=2] {'dom'}, use_global_device_ids=true, to_apply=%region_5.8 | all-reduce | flops 832 | bytes 6656 | tf_op jit(solution)/shard_map/psum | solution.py:91
  132.5 3.6 %all-reduce.3 = (f32[24,24]{1,0:T(8,128)S(1)}, f32[24,8]{0,1:T(8,128)S(1)}, f32[8,8]{0,1:T(8,128)S(1)}) all-reduce(f32[24,24]{1,0:T(8,128)S(1)} %get-tuple-element.11, f32[24,8]{0,1:T(8,128)S(1)} %get-tuple-element.12, f32[8,8]{0,1:T(8,128)S(1)} %get-tuple-element.13), channel_id=1, replica_groups=mesh['dom'=16,'spin'=2] {'spin'}, use_global_device_ids=true, to_apply=%region_6.9 | all-reduce | flops 832 | bytes 6656 | tf_op jit(solution)/shard_map/psum | solution.py:90
  136.3 1.2 convolution_subtract_fusion.1
  141.8 2.4 fusion.3
  144.1 5.6 %collective-permute-start.4 = (bf16[8,8,128]{2,1,0:T(8,128)(2,1)S(1)}, bf16[8,8,128]{2,1,0:T(8,128)(2,1)S(1)}, u32[]{:S(2)}, u32[]{:S(2)}) collective-permute-start(bf16[8,8,128]{2,1,0:T(8,128)(2,1)S(1)} %get-tuple-element.23), channel_id=1, source_target_pairs={{2,0},{4,2},{6,4},{8,6},{10,8},{12,10},{14,12},{16,14},{18,16},{20... | collective-permute-start | bytes 49160 | tf_op jit(solution)/shard_map/ppermute | solution.py:18
  150.4 1.0 collective-permute-done.3
  151.5 0.8 fusion.13
  152.3 1.4 copy.119
  153.7 7.5 %copy.73 = f32[8,1152,128]{2,0,1:T(8,128)} copy(f32[8,1152,128]{2,1,0:T(8,128)S(1)} %bitcast.121) | data formatting | bytes 9437184 | tf_op jit(solution)/shard_map/reshape | solution.py:80
  161.2 18.1 %gather_fusion.2 = f32[2048,8,128]{2,1,0:T(8,128)} fusion(f32[8,1152,128]{2,0,1:T(8,128)} %copy.73, s32[2048]{0:T(1024)S(1)} %fusion.43), kind=kCustom, calls=%fused_computation.2.clone | custom fusion | bytes 16785408 | tf_op jit(solution)/shard_map/jit(_take)/gather | solution.py:81
  179.3 9.1 %multiply_reduce_fusion = f32[8,128,128]{2,0,1:T(8,128)S(1)} fusion(f32[128,16]{1,0:T(8,128)S(1)} %fusion.25, f32[2048,8,128]{2,1,0:T(8,128)} %gather_fusion.2, pred[2048]{0:T(1024)(128)(4,1)S(1)} %compare_and_fusion), kind=kLoop, calls=%fused_computation.7 | loop fusion | flops 6160384 | bytes 8923136 | tf_op jit(solution)/shard_map/reduce_sum | solution.py:83
  188.5 1.6 gather_fusion.3
  190.3 1.0 fusion
  191.4 1.3 fusion.7
  192.7 1.9 fusion.4
  194.5 77.2 %all-reduce = (f32[32,32]{1,0:T(8,128)S(1)}, f32[32,8]{0,1:T(8,128)S(1)}, f32[8,8]{0,1:T(8,128)S(1)}) all-reduce(f32[32,32]{1,0:T(8,128)S(1)} %copy-done.6, f32[32,8]{0,1:T(8,128)S(1)} %fusion.4, f32[8,8]{0,1:T(8,128)S(1)} %fusion.7), channel_id=1, replica_groups=mesh['dom'=16,'spin'=2] {'dom'}, use_global_device_ids=true, to_apply=%region_14.19 | all-reduce | flops 1344 | bytes 10752 | tf_op jit(solution)/shard_map/psum | solution.py:91
  271.8 3.4 %all-reduce.2 = (f32[32,32]{1,0:T(8,128)S(1)}, f32[32,8]{0,1:T(8,128)S(1)}, f32[8,8]{0,1:T(8,128)S(1)}) all-reduce(f32[32,32]{1,0:T(8,128)S(1)} %get-tuple-element.8, f32[32,8]{0,1:T(8,128)S(1)} %get-tuple-element.9, f32[8,8]{0,1:T(8,128)S(1)} %get-tuple-element.10), channel_id=1, replica_groups=mesh['dom'=16,'spin'=2] {'spin'}, use_global_device_ids=true, to_apply=%region_15.20 | all-reduce | flops 1344 | bytes 10752 | tf_op jit(solution)/shard_map/psum | solution.py:90
  275.5 1.3 convolution_subtract_fusion
  280.6 1.4 convolution_bitcast_fusion
  (67 shorter events, 13.4 us)
Async XLA Ops:
  0.6 15.4 %copy-start = (bf16[8,128,128]{2,1,0:T(8,128)(2,1)S(1)}, bf16[8,128,128]{2,1,0:T(8,128)(2,1)}, u32[]{:S(2)}) copy-start(bf16[8,128,128]{2,1,0:T(8,128)(2,1)} %param.19) | copy-start | bytes 786436
  1.8 51.3 %collective-permute-start.2 = (bf16[8,128,128]{2,1,0:T(8,128)(2,1)S(1)}, bf16[8,128,128]{2,1,0:T(8,128)(2,1)S(1)}, u32[]{:S(2)}, u32[]{:S(2)}) collective-permute-start(bf16[8,128,128]{2,1,0:T(8,128)(2,1)S(1)} %bitcast.137), channel_id=1, source_target_pairs={{0,1},{1,0},{2,3},{3,2},{4,5},{5,4},{6,7},{7,6},{8,9},{9,8},{10,11... | collective-permute-start | bytes 786440 | tf_op jit(solution)/shard_map/ppermute | solution.py:32
  2.4 13.6 %collective-permute-start = (bf16[8,8,128]{2,1,0:T(8,128)(2,1)S(1)}, bf16[8,8,128]{2,1,0:T(8,128)(2,1)S(1)}, u32[]{:S(2)}, u32[]{:S(2)}) collective-permute-start(bf16[8,8,128]{2,1,0:T(8,128)(2,1)S(1)} %get-tuple-element.24), channel_id=1, source_target_pairs={{0,2},{2,4},{4,6},{6,8},{8,10},{10,12},{12,14},{14,16},{16,18},{18... | collective-permute-start | bytes 49160 | tf_op jit(solution)/shard_map/ppermute | solution.py:16
  5.0 11.1 %collective-permute-start.1 = (bf16[8,8,128]{2,1,0:T(8,128)(2,1)S(1)}, bf16[8,8,128]{2,1,0:T(8,128)(2,1)S(1)}, u32[]{:S(2)}, u32[]{:S(2)}) collective-permute-start(bf16[8,8,128]{2,1,0:T(8,128)(2,1)S(1)} %get-tuple-element.25), channel_id=1, source_target_pairs={{2,0},{4,2},{6,4},{8,6},{10,8},{12,10},{14,12},{16,14},{18,16},{20... | collective-permute-start | bytes 49160 | tf_op jit(solution)/shard_map/ppermute | solution.py:18
  43.9 11.0 %copy-start.1 = (f32[1,8,16384]{2,1,0:T(8,128)S(1)}, f32[1,8,16384]{2,1,0:T(8,128)}, u32[]{:S(2)}) copy-start(f32[1,8,16384]{2,1,0:T(8,128)} %param.16) | copy-start | bytes 1572868
  43.9 11.0 %copy-start.4 = (f32[1,16384]{1,0:T(1,128)S(1)}, f32[1,16384]{1,0:T(1,128)}, u32[]{:S(2)}) copy-start(f32[1,16384]{1,0:T(1,128)} %param.18) | copy-start | bytes 196612
  53.3 4.0 %copy-start.2 = (f32[1,16,16384]{2,1,0:T(8,128)S(1)}, f32[1,16,16384]{2,1,0:T(8,128)}, u32[]{:S(2)}) copy-start(f32[1,16,16384]{2,1,0:T(8,128)} %param.17) | copy-start | bytes 3145732
  54.9 4.0 %copy-start.5 = (f32[24,24]{1,0:T(8,128)S(1)}, f32[24,24]{1,0:T(8,128)}, u32[]{:S(2)}) copy-start(f32[24,24]{1,0:T(8,128)} %fusion.1) | copy-start | bytes 6916
  141.3 134.2 %copy-start.3 = (f32[8,16384]{1,0:T(8,128)}, f32[8,16384]{1,0:T(8,128)S(1)}, u32[]{:S(2)}) copy-start(f32[8,16384]{1,0:T(8,128)S(1)} %fusion.47) | copy-start | bytes 1572868
  141.4 47.1 %collective-permute-start.5 = (bf16[8,128,128]{2,0,1:T(8,128)(2,1)S(1)}, bf16[8,128,128]{2,0,1:T(8,128)(2,1)}, u32[]{:S(2)}, u32[]{:S(2)}) collective-permute-start(bf16[8,128,128]{2,0,1:T(8,128)(2,1)S(1)} %convert_bitcast_fusion), channel_id=1, source_target_pairs={{0,1},{1,0},{2,3},{3,2},{4,5},{5,4},{6,7},{7,6},{8,9},{9,8},{10,11... | collective-permute-start | bytes 786440 | tf_op jit(solution)/shard_map/ppermute | solution.py:32
  144.1 7.3 %collective-permute-start.3 = (bf16[8,8,128]{2,1,0:T(8,128)(2,1)S(1)}, bf16[8,8,128]{2,1,0:T(8,128)(2,1)S(1)}, u32[]{:S(2)}, u32[]{:S(2)}) collective-permute-start(bf16[8,8,128]{2,1,0:T(8,128)(2,1)S(1)} %get-tuple-element.22), channel_id=1, source_target_pairs={{0,2},{2,4},{4,6},{6,8},{8,10},{10,12},{12,14},{14,16},{16,18},{18... | collective-permute-start | bytes 49160 | tf_op jit(solution)/shard_map/ppermute | solution.py:16
  144.1 7.3 %collective-permute-start.4 = (bf16[8,8,128]{2,1,0:T(8,128)(2,1)S(1)}, bf16[8,8,128]{2,1,0:T(8,128)(2,1)S(1)}, u32[]{:S(2)}, u32[]{:S(2)}) collective-permute-start(bf16[8,8,128]{2,1,0:T(8,128)(2,1)S(1)} %get-tuple-element.23), channel_id=1, source_target_pairs={{2,0},{4,2},{6,4},{8,6},{10,8},{12,10},{14,12},{16,14},{18,16},{20... | collective-permute-start | bytes 49160 | tf_op jit(solution)/shard_map/ppermute | solution.py:18
  179.3 10.8 %copy-start.7 = (pred[128]{0:T(512)(128)(4,1)S(1)}, pred[128]{0:T(512)(128)(4,1)}, u32[]{:S(2)}) copy-start(pred[128]{0:T(512)(128)(4,1)} %get-tuple-element.20) | copy-start | bytes 388
  191.4 3.2 %copy-start.6 = (f32[32,32]{1,0:T(8,128)S(1)}, f32[32,32]{1,0:T(8,128)}, u32[]{:S(2)}) copy-start(f32[32,32]{1,0:T(8,128)} %fusion.3) | copy-start | bytes 12292
